TPU v7x, 32 devices: a whole 2x2x4 slice. The times are simulated.
32 devices in a mesh: grp: 2 (over y), dev: 16 (over z, x, core).
Axes of the slice: x: 2, y: 2, z: 4, core: 2. Of those that a mesh axis runs over, the one named last changes fastest.
Arguments:
- queries: float32 [128, 1024], P(('grp', 'dev')), may hold values from -4.5 to 4.5
- documents: float32 [4096, 1024], P(('grp', 'dev')), may hold values from -0.75 to 0.75
- doc_codes: int32 [4096, 128], P(('grp', 'dev')), may hold values from 0 to 255
- codebook: float32 [256, 1024], replicated, may hold values from -0.75 to 0.75
- candidate_owner: int32 [128, 32], P(('grp', 'dev')), may hold values from 0 to 31, all different within a row; in each aligned block of 4 rows (0 to 3, 4 to 7, ...) at most 4 rows name the same one
- candidate_local: int32 [128, 32], P(('grp', 'dev')), may hold values from 0 to 127
Outputs:
- codebook_gradient: float32 [256, 1024], P('dev', 'grp')
- query_loss: float32 [128], P(('grp', 'dev'))
Inputs may be any that keep to these rules, and one draw needn't show every extreme that they name: `candidate_owner`: each query names 32 different owners; among one device's 4 queries no owner is named more than 4 times, and in some device's queries one owner is named exactly 4 times.
All inputs are finite; a program needn't handle non-finite values.
Results may differ from a plain program's by a relative error of at most 0.0003.
Values sent between devices are 32-bit elements; how exact they have to be, the bound alone decides.
No kernel may reach another device: no remote copies, remote signals or barrier semaphores. Data moves between devices by JAX's collectives and lax.ppermute only.
A program may use at most 192 MiB of HBM per device.

v0:
```python
import jax
import jax.numpy as jnp
from jax import lax
from jax.sharding import PartitionSpec as P

D = 1024
M = 128
K = 256
C = 32
SUB = 8


def slot_positions(candidate_owner, capacity):
    owner_flat = candidate_owner.reshape(-1)
    ordinal = jnp.arange(owner_flat.shape[0], dtype=jnp.int32)
    earlier = (owner_flat[None, :] == owner_flat[:, None]) & (ordinal[None, :] < ordinal[:, None])
    rank_inside = jnp.sum(earlier.astype(jnp.int32), axis=1)
    return owner_flat * capacity + rank_inside


def distill(exact_score, student):
    teacher = jax.nn.softmax(exact_score, axis=-1)
    query_loss = jnp.sum(
        teacher * (jax.nn.log_softmax(exact_score, axis=-1) - jax.nn.log_softmax(student, axis=-1)),
        axis=-1,
    )
    weight = jax.nn.softmax(student, axis=-1) - teacher
    return (query_loss, weight)


def code_onehot(code_block):
    return (code_block[:, :, None] == jnp.arange(K, dtype=jnp.int32)[None, None, :]).astype(
        jnp.float32
    )


def fetched_terms(queries, vectors, code_rows, codebook):
    query_count = queries.shape[0]
    exact_score = jnp.einsum("qcd,qd->qc", vectors, queries, precision=lax.Precision.HIGHEST)
    query_parts = queries.reshape(query_count, M, SUB)
    lookup = jnp.einsum(
        "qmj,kmj->qmk", query_parts, codebook.reshape(K, M, SUB), precision=lax.Precision.HIGHEST
    )

    def student_one(pieces):
        code_one, lookup_one = pieces
        return jnp.einsum(
            "cmk,mk->c", code_onehot(code_one), lookup_one, precision=lax.Precision.HIGHEST
        )

    student = lax.map(student_one, (code_rows, lookup))
    query_loss, weight = distill(exact_score, student)

    def table_one(pieces):
        code_one, weight_one = pieces
        return jnp.einsum(
            "cmk,c->mk", code_onehot(code_one), weight_one, precision=lax.Precision.HIGHEST
        )

    weight_table = lax.map(table_one, (code_rows, weight))
    gradient = jnp.einsum(
        "qmk,qmj->kmj", weight_table, query_parts, precision=lax.Precision.HIGHEST
    )
    return (query_loss, gradient.reshape(K, D))


def shards(queries, documents, doc_codes, codebook, candidate_owner, candidate_local):
    groups = lax.axis_size("grp")
    owners = lax.axis_size("dev")
    query_count = queries.shape[0]
    capacity = min(query_count, max(2, 2 * query_count * C // (groups * owners)))
    slot_count = groups * owners * capacity
    positions = slot_positions(candidate_owner, capacity)
    wanted = jnp.zeros((slot_count,), jnp.int32).at[positions].set(candidate_local.reshape(-1))
    asked = lax.all_to_all(
        lax.all_to_all(
            wanted.reshape(groups, owners, capacity), "grp", split_axis=0, concat_axis=0, tiled=True
        ),
        "dev",
        split_axis=1,
        concat_axis=1,
        tiled=True,
    )
    doc_index = asked.reshape(slot_count)
    found_rows = documents[doc_index].reshape(groups, owners, capacity, D)
    found_codes = doc_codes[doc_index].astype(jnp.float32).reshape(groups, owners, capacity, M)
    fetched, fetched_codes = (
        lax.all_to_all(
            lax.all_to_all(found_rows, "grp", split_axis=0, concat_axis=0, tiled=True),
            "dev",
            split_axis=1,
            concat_axis=1,
            tiled=True,
        ),
        lax.all_to_all(
            lax.all_to_all(found_codes, "grp", split_axis=0, concat_axis=0, tiled=True),
            "dev",
            split_axis=1,
            concat_axis=1,
            tiled=True,
        ),
    )
    vectors = fetched.reshape(slot_count, D)[positions].reshape(query_count, C, D)
    code_rows = (
        fetched_codes.reshape(slot_count, M)[positions].astype(jnp.int32).reshape(query_count, C, M)
    )
    query_loss, local_gradient = fetched_terms(queries, vectors, code_rows, codebook)
    partial_sum = lax.psum_scatter(local_gradient, "dev", scatter_dimension=0, tiled=True)
    codebook_gradient = lax.psum_scatter(partial_sum, "grp", scatter_dimension=1, tiled=True)
    return (codebook_gradient, query_loss)


def solution(mesh):
    in_specs = (
        P(("grp", "dev"), None),
        P(("grp", "dev"), None),
        P(("grp", "dev"), None),
        P(),
        P(("grp", "dev"), None),
        P(("grp", "dev"), None),
    )
    out_specs = (P("dev", "grp"), P(("grp", "dev")))
    return jax.shard_map(shards, mesh=mesh, in_specs=in_specs, out_specs=out_specs, check_vma=False)
```

profile of v0, /device:TPU:0, one launch (start us, length us, event | category | flops | bytes accessed | tf_op | source)
XLA Modules:
  0.0 180.2 jit_solution(6461381742338682574)
XLA Ops:
  11.0 7.8 %all_to_all.30 = s32[2,16,4]{1,2,0:T(4,128)S(1)} all-to-all(s32[2,16,4]{1,2,0:T(4,128)S(1)} %copy.46), channel_id=1, replica_groups=mesh['grp'=2,'dev'=16] {'grp'}, dimensions={0} | all-to-all | bytes 1024 | tf_op jit(solution)/shard_map/all_to_all | solution.py:76
  18.9 12.2 %all_to_all.31 = s32[2,16,4]{2,0,1:T(2,128)S(1)} all-to-all(s32[2,16,4]{2,0,1:T(2,128)S(1)} %copy.47), channel_id=1, replica_groups=mesh['grp'=2,'dev'=16] {'dev'}, dimensions={1} | all-to-all | bytes 1024 | tf_op jit(solution)/shard_map/all_to_all | solution.py:75
  31.2 1.5 gather_fusion
  32.7 6.5 %all_to_all.32 = f32[2,16,4,128]{3,2,1,0:T(4,128)S(1)} all-to-all(f32[2,16,4,128]{3,2,1,0:T(4,128)S(1)} %bitcast.63), channel_id=1, replica_groups=mesh['grp'=2,'dev'=16] {'grp'}, dimensions={0} | all-to-all | bytes 131072 | tf_op jit(solution)/shard_map/all_to_all | solution.py:96
  39.8 3.5 %all-to-all-start.3 = ((f32[2,16,4,128]{3,2,0,1:T(4,128)}), f32[2,16,4,128]{3,2,0,1:T(4,128)S(1)}, u32[]{:S(2)}, u32[]{:S(2)}) async-start(f32[2,16,4,128]{3,2,0,1:T(4,128)} %copy.49), calls=%async_computation.3 | async-start | bytes 131072 | tf_op jit(solution)/shard_map/all_to_all | solution.py:95
  45.7 4.5 %all-to-all-done.3 = f32[2,16,4,128]{3,2,0,1:T(4,128)S(1)} async-done(((f32[2,16,4,128]{3,2,0,1:T(4,128)}), f32[2,16,4,128]{3,2,0,1:T(4,128)S(1)}, u32[]{:S(2)}, u32[]{:S(2)}) %all-to-all-start.3) | async-done | bytes 65568 | tf_op jit(solution)/shard_map/all_to_all | solution.py:95
  50.2 3.5 %all-to-all-start.4 = ((f32[2,16,4,1024]{3,2,1,0:T(4,128)}), f32[2,16,4,1024]{3,2,1,0:T(4,128)S(1)}, u32[]{:S(2)}, u32[]{:S(2)}) async-start(f32[2,16,4,1024]{3,2,1,0:T(4,128)} %reshape.118), calls=%async_computation.4 | async-start | bytes 1048576 | tf_op jit(solution)/shard_map/all_to_all | solution.py:89
  55.5 6.1 %all-to-all-done.4 = f32[2,16,4,1024]{3,2,1,0:T(4,128)S(1)} async-done(((f32[2,16,4,1024]{3,2,1,0:T(4,128)}), f32[2,16,4,1024]{3,2,1,0:T(4,128)S(1)}, u32[]{:S(2)}, u32[]{:S(2)}) %all-to-all-start.4) | async-done | bytes 524320 | tf_op jit(solution)/shard_map/all_to_all | solution.py:89
  62.5 3.6 %all-to-all-start.5 = ((f32[2,16,4,1024]{3,2,0,1:T(4,128)}), f32[2,16,4,1024]{3,2,0,1:T(4,128)S(1)}, u32[]{:S(2)}, u32[]{:S(2)}) async-start(f32[2,16,4,1024]{3,2,0,1:T(4,128)} %copy.54), calls=%async_computation.5 | async-start | bytes 1048576 | tf_op jit(solution)/shard_map/all_to_all | solution.py:88
  66.1 6.7 %while.20 = (s32[]{:T(128)}, f32[4,32]{1,0:T(4,128)S(1)}, s32[4,32,128]{2,1,0:T(8,128)S(1)}, f32[4,128,256]{2,0,1:T(4,128)S(1)}, s32[]{:T(128)}, /*index=5*/s32[]{:T(128)}) while((s32[]{:T(128)}, f32[4,32]{1,0:T(4,128)S(1)}, s32[4,32,128]{2,1,0:T(8,128)S(1)}, f32[4,128,256]{2,0,1:T(4,128)S(1)}, s32[]{:T(128)}, /*index=5*/s32[]{:T(128)}) %tuple.53), condition=%wide.region_3.4_spmd, body=%wide.region_2.3_spmd.sunk | while | flops 3145698 | bytes 704977 | solution.py:51
  66.3 1.5 select_reduce_fusion.2
  71.4 1.5 select_reduce_fusion.2
  73.0 7.5 %all-to-all-done.5 = f32[2,16,4,1024]{3,2,0,1:T(4,128)S(1)} async-done(((f32[2,16,4,1024]{3,2,0,1:T(4,128)}), f32[2,16,4,1024]{3,2,0,1:T(4,128)S(1)}, u32[]{:S(2)}, u32[]{:S(2)}) %all-to-all-start.5) | async-done | bytes 524320 | tf_op jit(solution)/shard_map/all_to_all | solution.py:88
  83.2 19.7 %while.21 = (s32[]{:T(128)}, f32[4,128,256]{2,0,1:T(4,128)S(1)}, s32[4,32,128]{2,1,0:T(8,128)S(1)}, f32[4,32]{1,0:T(4,128)S(1)}, s32[]{:T(128)}, /*index=5*/s32[]{:T(128)}) while((s32[]{:T(128)}, f32[4,128,256]{2,0,1:T(4,128)S(1)}, s32[4,32,128]{2,1,0:T(8,128)S(1)}, f32[4,32]{1,0:T(4,128)S(1)}, s32[]{:T(128)}, /*index=5*/s32[]{:T(128)}) %tuple.55), condition=%wide.region_9.10_spmd, body=%wide.region_8.9_spmd.sunk | while | flops 13631490 | bytes 2540113 | solution.py:60
  84.1 2.2 %fusion.21 = f32[1,128,256]{2,0,1:T(1,128)S(1)} fusion(pred[32,128,256]{2,1,0:T(32,128)(4,1)S(1)} %iota_compare_fusion.4, f32[4,32]{1,0:T(4,128)S(1)} %get-tuple-element.172, s32[]{:T(128)} %get-tuple-element.163), kind=kOutput, calls=%fused_computation.6.clone.1 | convolution fusion | flops 12582912 | bytes 1180164 | tf_op jit(solution)/shard_map/while/body/eval_jaxpr/cmk,c->mk/dot_general | solution.py:56
  86.2 1.8 %dynamic_update_slice.11 = f32[4,128,256]{2,0,1:T(4,128)S(1)} dynamic-update-slice(f32[4,128,256]{2,0,1:T(4,128)S(1)} %get-tuple-element.164, f32[1,128,256]{2,0,1:T(1,128)S(1)} %fusion.21, s32[]{:T(128)} %get-tuple-element.163, s32[]{:T(128)} %constant.21.clone.1..sunk.1, s32[]{:T(128)} %constant.21.clone.1..sunk.1) | dynamic-update-slice | bytes 262148 | tf_op jit(solution)/shard_map/while/body/jit(dynamic_update_index_in_dim)/dynamic_update_slice | solution.py:60
  89.0 2.2 %fusion.21 = f32[1,128,256]{2,0,1:T(1,128)S(1)} fusion(pred[32,128,256]{2,1,0:T(32,128)(4,1)S(1)} %iota_compare_fusion.4, f32[4,32]{1,0:T(4,128)S(1)} %get-tuple-element.172, s32[]{:T(128)} %get-tuple-element.163), kind=kOutput, calls=%fused_computation.6.clone.1 | convolution fusion | flops 12582912 | bytes 1180164 | tf_op jit(solution)/shard_map/while/body/eval_jaxpr/cmk,c->mk/dot_general | solution.py:56
  91.2 1.8 %dynamic_update_slice.11 = f32[4,128,256]{2,0,1:T(4,128)S(1)} dynamic-update-slice(f32[4,128,256]{2,0,1:T(4,128)S(1)} %get-tuple-element.164, f32[1,128,256]{2,0,1:T(1,128)S(1)} %fusion.21, s32[]{:T(128)} %get-tuple-element.163, s32[]{:T(128)} %constant.21.clone.1..sunk.1, s32[]{:T(128)} %constant.21.clone.1..sunk.1) | dynamic-update-slice | bytes 262148 | tf_op jit(solution)/shard_map/while/body/jit(dynamic_update_index_in_dim)/dynamic_update_slice | solution.py:60
  93.9 2.2 %fusion.21 = f32[1,128,256]{2,0,1:T(1,128)S(1)} fusion(pred[32,128,256]{2,1,0:T(32,128)(4,1)S(1)} %iota_compare_fusion.4, f32[4,32]{1,0:T(4,128)S(1)} %get-tuple-element.172, s32[]{:T(128)} %get-tuple-element.163), kind=kOutput, calls=%fused_computation.6.clone.1 | convolution fusion | flops 12582912 | bytes 1180164 | tf_op jit(solution)/shard_map/while/body/eval_jaxpr/cmk,c->mk/dot_general | solution.py:56
  96.1 1.8 %dynamic_update_slice.11 = f32[4,128,256]{2,0,1:T(4,128)S(1)} dynamic-update-slice(f32[4,128,256]{2,0,1:T(4,128)S(1)} %get-tuple-element.164, f32[1,128,256]{2,0,1:T(1,128)S(1)} %fusion.21, s32[]{:T(128)} %get-tuple-element.163, s32[]{:T(128)} %constant.21.clone.1..sunk.1, s32[]{:T(128)} %constant.21.clone.1..sunk.1) | dynamic-update-slice | bytes 262148 | tf_op jit(solution)/shard_map/while/body/jit(dynamic_update_index_in_dim)/dynamic_update_slice | solution.py:60
  98.9 2.2 %fusion.21 = f32[1,128,256]{2,0,1:T(1,128)S(1)} fusion(pred[32,128,256]{2,1,0:T(32,128)(4,1)S(1)} %iota_compare_fusion.4, f32[4,32]{1,0:T(4,128)S(1)} %get-tuple-element.172, s32[]{:T(128)} %get-tuple-element.163), kind=kOutput, calls=%fused_computation.6.clone.1 | convolution fusion | flops 12582912 | bytes 1180164 | tf_op jit(solution)/shard_map/while/body/eval_jaxpr/cmk,c->mk/dot_general | solution.py:56
  101.0 1.8 %dynamic_update_slice.11 = f32[4,128,256]{2,0,1:T(4,128)S(1)} dynamic-update-slice(f32[4,128,256]{2,0,1:T(4,128)S(1)} %get-tuple-element.164, f32[1,128,256]{2,0,1:T(1,128)S(1)} %fusion.21, s32[]{:T(128)} %get-tuple-element.163, s32[]{:T(128)} %constant.21.clone.1..sunk.1, s32[]{:T(128)} %constant.21.clone.1..sunk.1) | dynamic-update-slice | bytes 262148 | tf_op jit(solution)/shard_map/while/body/jit(dynamic_update_index_in_dim)/dynamic_update_slice | solution.py:60
  105.7 55.9 %reduce-scatter.3.cloned.1.call-done = f32[16,1024]{1,0:T(8,128)} async-done(((f32[256,1024]{1,0:T(8,128)}), f32[16,1024]{1,0:T(8,128)}) %reduce-scatter.3.cloned.1.call-update) | async-done | bytes 65552 | tf_op jit(solution)/shard_map/reduce_scatter | solution.py:108
  161.6 11.7 %reduce-scatter.5.cloned.1.call-done = f32[16,512]{1,0:T(8,128)} async-done(((f32[16,1024]{1,0:T(8,128)}), f32[16,512]{1,0:T(8,128)}) %reduce-scatter.5.cloned.1.call-update) | async-done | bytes 32784 | tf_op jit(solution)/shard_map/reduce_scatter | solution.py:109
  (78 shorter events, 22.2 us)
Async XLA Ops:
  7.2 36.7 %copy-start = (f32[128,1024]{1,0:T(8,128)S(1)}, f32[128,1024]{1,0:T(8,128)}, u32[]{:S(2)}) copy-start(f32[128,1024]{1,0:T(8,128)} %param.12) | copy-start | bytes 1572868
  7.2 36.2 %copy-start.3 = (f32[4,1024]{1,0:T(4,128)S(1)}, f32[4,1024]{1,0:T(4,128)}, u32[]{:S(2)}) copy-start(f32[4,1024]{1,0:T(4,128)} %param.11) | copy-start | bytes 49156
  7.2 36.4 %copy-start.1 = (f32[256,1024]{1,0:T(8,128)S(1)}, f32[256,1024]{1,0:T(8,128)}, u32[]{:S(2)}) copy-start(f32[256,1024]{1,0:T(8,128)} %param.14) | copy-start | bytes 3145732
  39.8 10.4 %all-to-all-start.3 = ((f32[2,16,4,128]{3,2,0,1:T(4,128)}), f32[2,16,4,128]{3,2,0,1:T(4,128)S(1)}, u32[]{:S(2)}, u32[]{:S(2)}) async-start(f32[2,16,4,128]{3,2,0,1:T(4,128)} %copy.49), calls=%async_computation.3 | async-start | bytes 131072 | tf_op jit(solution)/shard_map/all_to_all | solution.py:95
  50.2 11.5 %all-to-all-start.4 = ((f32[2,16,4,1024]{3,2,1,0:T(4,128)}), f32[2,16,4,1024]{3,2,1,0:T(4,128)S(1)}, u32[]{:S(2)}, u32[]{:S(2)}) async-start(f32[2,16,4,1024]{3,2,1,0:T(4,128)} %reshape.118), calls=%async_computation.4 | async-start | bytes 1048576 | tf_op jit(solution)/shard_map/all_to_all | solution.py:89
  62.5 18.0 %all-to-all-start.5 = ((f32[2,16,4,1024]{3,2,0,1:T(4,128)}), f32[2,16,4,1024]{3,2,0,1:T(4,128)S(1)}, u32[]{:S(2)}, u32[]{:S(2)}) async-start(f32[2,16,4,1024]{3,2,0,1:T(4,128)} %copy.54), calls=%async_computation.5 | async-start | bytes 1048576 | tf_op jit(solution)/shard_map/all_to_all | solution.py:88
  66.1 95.5 %reduce-scatter.3.cloned.1.call-start = ((), (), s32[]{:S(2)}) async-start(), calls=%async_computation.8 | async-start | bytes 1114112 | tf_op jit(solution)/shard_map/reduce_scatter | solution.py:108
  80.7 2.5 %copy-start.2 = (f32[4,128,256]{2,0,1:T(4,128)S(1)}, f32[4,128,256]{2,0,1:T(4,128)}, u32[]{:S(2)}) copy-start(f32[4,128,256]{2,0,1:T(4,128)} %custom-call.9) | copy-start | bytes 1572868
  105.6 67.8 %reduce-scatter.5.cloned.1.call-start = ((), (), s32[]{:S(2)}) async-start(), calls=%async_computation.9 | async-start | bytes 98304 | tf_op jit(solution)/shard_map/reduce_scatter | solution.py:109
Sparse Core Ops, SparseCore 0:
  105.7 55.8 reduce-scatter.2
  164.5 8.8 reduce-scatter.4
where the time goes:
time: 181 us; the launch traced here: 180 us
  waiting for transfers between devices  85.9 us (47%)
  blocking collectives  26.5 us (15%)
  local copies, waits for them, and re-layouts  19.3 us (11%)
  between operations  14.3 us (8%)
  matrix products  11.8 us (7%)
  other arithmetic  11.6 us (6%)
  starting transfers between devices  10.6 us (6%)
    reduce_scatter x1, waiting for transfers between devices, shards(): lax.psum_scatter(local_gradient, 'dev', scatter_dimension=0, tiled=True)  55.9 us
    all_to_all x1, blocking collectives, shards(): lax.all_to_all(lax.all_to_all(wanted.reshape(groups, owners, capacity), '...  12.2 us
    reduce_scatter x1, waiting for transfers between devices, shards(): lax.psum_scatter(partial_sum, 'grp', scatter_dimension=1, tiled=True)  11.7 us
    dot_general x4, matrix products, table_one(): jnp.einsum('cmk,c->mk', code_onehot(code_one), weight_one, precision=lax....  8.72 us
    all_to_all x1, blocking collectives, shards(): lax.all_to_all(wanted.reshape(groups, owners, capacity), 'grp', split_axi...  7.82 us
    all_to_all x1, waiting for transfers between devices, shards(): lax.all_to_all(lax.all_to_all(found_rows, 'grp', split_axis=0, concat_axi...  7.51 us
    dynamic_update_slice x4, local copies, waits for them, and re-layouts, fetched_terms(): weight_table = lax.map(table_one, (code_rows, weight))  7.34 us
    all_to_all x1, blocking collectives, shards(): lax.all_to_all(found_codes, 'grp', split_axis=0, concat_axis=0, tiled=True)  6.5 us
  transfers between devices with their start and end apart: 5, of which 5 were waited for; matrix products, arithmetic and copies ran while one was open for 6% of the time, Pallas kernels for 0%

commit v1 on v0

--- a/solution.py
+++ b/solution.py
@@ -84,6 +84,29 @@
     doc_index = asked.reshape(slot_count)
     found_rows = documents[doc_index].reshape(groups, owners, capacity, D)
     found_codes = doc_codes[doc_index].astype(jnp.float32).reshape(groups, owners, capacity, M)
+
+    def advance_state(view):
+        axis_name = "dev"
+        t1 = jax.lax.psum(1, axis_name)
+        long_array = jax.lax.axis_index(axis_name)
+        taken_in, tile_out = (t1, long_array)
+        front = view.shape[1] // taken_in
+        response = list(view.shape)
+        response[1] = front
+        left_arr = response[1]
+        response[1] = left_arr * taken_in
+        right_arr = jnp.zeros(response, view.dtype)
+        for c in range(taken_in):
+            piece_next = lax.dynamic_slice_in_dim(view, (tile_out ^ c) * front, front, axis=1)
+            if c:
+                piece_next = jax.lax.ppermute(
+                    piece_next, axis_name, tuple(((it, it ^ c) for it in range(taken_in)))
+                )
+            right_arr = lax.dynamic_update_slice_in_dim(
+                right_arr, piece_next, (tile_out ^ c) * left_arr, axis=1
+            )
+        return right_arr
+
     fetched, fetched_codes = (
         lax.all_to_all(
             lax.all_to_all(found_rows, "grp", split_axis=0, concat_axis=0, tiled=True),
@@ -92,13 +115,7 @@
             concat_axis=1,
             tiled=True,
         ),
-        lax.all_to_all(
-            lax.all_to_all(found_codes, "grp", split_axis=0, concat_axis=0, tiled=True),
-            "dev",
-            split_axis=1,
-            concat_axis=1,
-            tiled=True,
-        ),
+        advance_state(lax.all_to_all(found_codes, "grp", split_axis=0, concat_axis=0, tiled=True)),
     )
     vectors = fetched.reshape(slot_count, D)[positions].reshape(query_count, C, D)
     code_rows = (

time: 181 us -> 192 us (1.061)
  starting transfers between devices: 10.6 us -> 38.8 us
  blocking collectives: 26.5 us -> 7.82 us
    ppermute x0 -> x15, starting transfers between devices: none -> 20.5 us  [advance_state(): jax.lax.ppermute(piece_next, axis_name, tuple(((it, it ^ c) for it in ran...]
    all_to_all x2 -> x0, blocking collectives: 18.7 us -> none  [the longest x1 12.2 us: shards(): lax.all_to_all(lax.all_to_all(wanted.reshape(groups, owners, capacity), '...]
    all_to_all x1, waiting for transfers between devices: 6.14 us -> 0.01 us  [shards(): lax.all_to_all(found_rows, 'grp', split_axis=0, concat_axis=0, tiled=True)]
    all_to_all x1 -> x2, starting transfers between devices: 3.49 us -> 9.2 us  [the longest x1 5.91 us: shards(): lax.all_to_all(lax.all_to_all(wanted.reshape(groups, owners, capacity), '...]
    all_to_all x1 -> x2, waiting for transfers between devices: 4.53 us -> 6.87 us  [the longest x1 4 us: shards(): lax.all_to_all(lax.all_to_all(wanted.reshape(groups, owners, capacity), '...]
  transfers between devices with their start and end apart: 5 -> 21, of which waited for: 5 -> 7; matrix products, arithmetic and copies ran while one was open for 6% -> 7% of each run, Pallas kernels for 0% -> 0%
where the time goes in v1:
time: 192 us; the launch traced here: 191 us
  waiting for transfers between devices  85.4 us (44%)
  starting transfers between devices  38.8 us (20%)
  local copies, waits for them, and re-layouts  20.5 us (11%)
  between operations  14.4 us (8%)
  other arithmetic  12.2 us (6%)
  matrix products  11.8 us (6%)
  blocking collectives  7.82 us (4%)
    reduce_scatter x1, waiting for transfers between devices, shards(): lax.psum_scatter(local_gradient, 'dev', scatter_dimension=0, tiled=True)  57.4 us
    ppermute x15, starting transfers between devices, advance_state(): jax.lax.ppermute(piece_next, axis_name, tuple(((it, it ^ c) for it in ran...  20.5 us
    reduce_scatter x1, waiting for transfers between devices, shards(): lax.psum_scatter(partial_sum, 'grp', scatter_dimension=1, tiled=True)  11.7 us
    dot_general x4, matrix products, table_one(): jnp.einsum('cmk,c->mk', code_onehot(code_one), weight_one, precision=lax....  8.72 us
    all_to_all x1, blocking collectives, shards(): lax.all_to_all(wanted.reshape(groups, owners, capacity), 'grp', split_axi...  7.82 us
    all_to_all x1, waiting for transfers between devices, shards(): lax.all_to_all(lax.all_to_all(found_rows, 'grp', split_axis=0, concat_axi...  7.56 us
    dynamic_update_slice x4, local copies, waits for them, and re-layouts, fetched_terms(): weight_table = lax.map(table_one, (code_rows, weight))  7.34 us
    dot_general x4, other arithmetic, student_one(): jnp.einsum('cmk,mk->c', code_onehot(code_one), lookup_one, precision=lax....  5.94 us
  transfers between devices with their start and end apart: 21, of which 7 were waited for; matrix products, arithmetic and copies ran while one was open for 7% of the time, Pallas kernels for 0%

profile of v1, /device:TPU:0, one launch (start us, length us, event | category | flops | bytes accessed | tf_op | source)
XLA Modules:
  0.0 191.1 jit_solution(11485682397129573600)
XLA Ops:
  10.9 7.8 %all_to_all.25 = s32[2,16,4]{1,2,0:T(4,128)S(1)} all-to-all(s32[2,16,4]{1,2,0:T(4,128)S(1)} %copy.42), channel_id=1, replica_groups=mesh['grp'=2,'dev'=16] {'grp'}, dimensions={0} | all-to-all | bytes 1024 | tf_op jit(solution)/shard_map/all_to_all | solution.py:76
  19.4 5.9 %all-to-all-start.1 = ((s32[2,16,4]{2,0,1:T(2,128)}), s32[2,16,4]{2,0,1:T(2,128)S(1)}, u32[]{:S(2)}, u32[]{:S(2)}) async-start(s32[2,16,4]{2,0,1:T(2,128)} %copy.43), calls=%async_computation.1 | async-start | bytes 32768 | tf_op jit(solution)/shard_map/all_to_all | solution.py:75
  27.8 4.0 %all-to-all-done.1 = s32[2,16,4]{2,0,1:T(2,128)S(1)} async-done(((s32[2,16,4]{2,0,1:T(2,128)}), s32[2,16,4]{2,0,1:T(2,128)S(1)}, u32[]{:S(2)}, u32[]{:S(2)}) %all-to-all-start.1) | async-done | bytes 544 | tf_op jit(solution)/shard_map/all_to_all | solution.py:75
  33.3 3.3 %all-to-all-start.2 = ((f32[2,16,4,128]{3,2,1,0:T(4,128)}), f32[2,16,4,128]{3,2,1,0:T(4,128)S(1)}, u32[]{:S(2)}, u32[]{:S(2)}) async-start(f32[2,16,4,128]{3,2,1,0:T(4,128)} %bitcast.13), calls=%async_computation.2 | async-start | bytes 131072 | tf_op jit(solution)/shard_map/all_to_all | solution.py:118
  37.8 2.9 %all-to-all-done.2 = f32[2,16,4,128]{3,2,1,0:T(4,128)S(1)} async-done(((f32[2,16,4,128]{3,2,1,0:T(4,128)}), f32[2,16,4,128]{3,2,1,0:T(4,128)S(1)}, u32[]{:S(2)}, u32[]{:S(2)}) %all-to-all-start.2) | async-done | bytes 65568 | tf_op jit(solution)/shard_map/all_to_all | solution.py:118
  42.6 3.5 %all-to-all-start.3 = ((f32[2,16,4,1024]{3,2,1,0:T(4,128)}), f32[2,16,4,1024]{3,2,1,0:T(4,128)S(1)}, u32[]{:S(2)}, u32[]{:S(2)}) async-start(f32[2,16,4,1024]{3,2,1,0:T(4,128)} %reshape.118), calls=%async_computation.3 | async-start | bytes 1048576 | tf_op jit(solution)/shard_map/all_to_all | solution.py:112
  50.2 2.2 %collective-permute-start.6 = (f32[2,1,4,128]{3,2,1,0:T(4,128)S(1)}, f32[2,1,4,128]{3,2,1,0:T(4,128)S(1)}, u32[]{:S(2)}, u32[]{:S(2)}) collective-permute-start(f32[2,1,4,128]{3,2,1,0:T(4,128)S(1)} %get-tuple-element.93), channel_id=1, source_target_pairs={{0,7},{1,6},{2,5},{3,4},{4,3},{5,2},{6,1},{7,0},{8,15},{9,14},{10,... | collective-permute-start | bytes 12296 | tf_op jit(solution)/shard_map/ppermute | solution.py:102
  52.9 2.1 %collective-permute-start.8 = (f32[2,1,4,128]{3,2,1,0:T(4,128)S(1)}, f32[2,1,4,128]{3,2,1,0:T(4,128)S(1)}, u32[]{:S(2)}, u32[]{:S(2)}) collective-permute-start(f32[2,1,4,128]{3,2,1,0:T(4,128)S(1)} %get-tuple-element.91), channel_id=1, source_target_pairs={{0,9},{1,8},{2,11},{3,10},{4,13},{5,12},{6,15},{7,14},{8,1},{9,0},... | collective-permute-start | bytes 12296 | tf_op jit(solution)/shard_map/ppermute | solution.py:102
  55.6 3.1 %collective-permute-start.10 = (f32[2,1,4,128]{3,2,1,0:T(4,128)S(1)}, f32[2,1,4,128]{3,2,1,0:T(4,128)S(1)}, u32[]{:S(2)}, u32[]{:S(2)}) collective-permute-start(f32[2,1,4,128]{3,2,1,0:T(4,128)S(1)} %get-tuple-element.89), channel_id=1, source_target_pairs={{0,11},{1,10},{2,9},{3,8},{4,15},{5,14},{6,13},{7,12},{8,3},{9,2},... | collective-permute-start | bytes 12296 | tf_op jit(solution)/shard_map/ppermute | solution.py:102
  59.2 3.0 %collective-permute-start.12 = (f32[2,1,4,128]{3,2,1,0:T(4,128)S(1)}, f32[2,1,4,128]{3,2,1,0:T(4,128)S(1)}, u32[]{:S(2)}, u32[]{:S(2)}) collective-permute-start(f32[2,1,4,128]{3,2,1,0:T(4,128)S(1)} %get-tuple-element.87), channel_id=1, source_target_pairs={{0,13},{1,12},{2,15},{3,14},{4,9},{5,8},{6,11},{7,10},{8,5},{9,4},... | collective-permute-start | bytes 12296 | tf_op jit(solution)/shard_map/ppermute | solution.py:102
  62.8 3.9 %collective-permute-start.14 = (f32[2,1,4,128]{3,2,1,0:T(4,128)S(1)}, f32[2,1,4,128]{3,2,1,0:T(4,128)S(1)}, u32[]{:S(2)}, u32[]{:S(2)}) collective-permute-start(f32[2,1,4,128]{3,2,1,0:T(4,128)S(1)} %get-tuple-element.85), channel_id=1, source_target_pairs={{0,15},{1,14},{2,13},{3,12},{4,11},{5,10},{6,9},{7,8},{8,7},{9,6},... | collective-permute-start | bytes 12296 | tf_op jit(solution)/shard_map/ppermute | solution.py:102
  70.1 5.5 %all-to-all-start.4 = ((f32[2,16,4,1024]{3,2,0,1:T(4,128)}), f32[2,16,4,1024]{3,2,0,1:T(4,128)S(1)}, u32[]{:S(2)}, u32[]{:S(2)}) async-start(f32[2,16,4,1024]{3,2,0,1:T(4,128)} %copy.48), calls=%async_computation.4 | async-start | bytes 1048576 | tf_op jit(solution)/shard_map/all_to_all | solution.py:111
  75.6 6.7 %while.20 = (s32[]{:T(128)}, f32[4,32]{1,0:T(4,128)S(1)}, s32[4,32,128]{2,1,0:T(8,128)S(1)}, f32[4,128,256]{2,0,1:T(4,128)S(1)}, s32[]{:T(128)}, /*index=5*/s32[]{:T(128)}) while((s32[]{:T(128)}, f32[4,32]{1,0:T(4,128)S(1)}, s32[4,32,128]{2,1,0:T(8,128)S(1)}, f32[4,128,256]{2,0,1:T(4,128)S(1)}, s32[]{:T(128)}, /*index=5*/s32[]{:T(128)}) %tuple.68), condition=%wide.region_3.4_spmd, body=%wide.region_2.3_spmd.sunk | while | flops 3145698 | bytes 704977 | solution.py:51
  82.5 7.6 %all-to-all-done.4 = f32[2,16,4,1024]{3,2,0,1:T(4,128)S(1)} async-done(((f32[2,16,4,1024]{3,2,0,1:T(4,128)}), f32[2,16,4,1024]{3,2,0,1:T(4,128)S(1)}, u32[]{:S(2)}, u32[]{:S(2)}) %all-to-all-start.4) | async-done | bytes 524320 | tf_op jit(solution)/shard_map/all_to_all | solution.py:111
  92.7 19.7 %while.21 = (s32[]{:T(128)}, f32[4,128,256]{2,0,1:T(4,128)S(1)}, s32[4,32,128]{2,1,0:T(8,128)S(1)}, f32[4,32]{1,0:T(4,128)S(1)}, s32[]{:T(128)}, /*index=5*/s32[]{:T(128)}) while((s32[]{:T(128)}, f32[4,128,256]{2,0,1:T(4,128)S(1)}, s32[4,32,128]{2,1,0:T(8,128)S(1)}, f32[4,32]{1,0:T(4,128)S(1)}, s32[]{:T(128)}, /*index=5*/s32[]{:T(128)}) %tuple.69), condition=%wide.region_9.10_spmd, body=%wide.region_8.9_spmd.sunk | while | flops 13631490 | bytes 2540113 | solution.py:60
  93.6 2.2 %fusion.21 = f32[1,128,256]{2,0,1:T(1,128)S(1)} fusion(pred[32,128,256]{2,1,0:T(32,128)(4,1)S(1)} %iota_compare_fusion.4, f32[4,32]{1,0:T(4,128)S(1)} %get-tuple-element.188, s32[]{:T(128)} %get-tuple-element.179), kind=kOutput, calls=%fused_computation.6.clone.1 | convolution fusion | flops 12582912 | bytes 1180164 | tf_op jit(solution)/shard_map/while/body/eval_jaxpr/cmk,c->mk/dot_general | solution.py:56
  95.8 1.8 dynamic_update_slice.91
  98.5 2.2 %fusion.21 = f32[1,128,256]{2,0,1:T(1,128)S(1)} fusion(pred[32,128,256]{2,1,0:T(32,128)(4,1)S(1)} %iota_compare_fusion.4, f32[4,32]{1,0:T(4,128)S(1)} %get-tuple-element.188, s32[]{:T(128)} %get-tuple-element.179), kind=kOutput, calls=%fused_computation.6.clone.1 | convolution fusion | flops 12582912 | bytes 1180164 | tf_op jit(solution)/shard_map/while/body/eval_jaxpr/cmk,c->mk/dot_general | solution.py:56
  100.7 1.8 dynamic_update_slice.91
  103.5 2.2 %fusion.21 = f32[1,128,256]{2,0,1:T(1,128)S(1)} fusion(pred[32,128,256]{2,1,0:T(32,128)(4,1)S(1)} %iota_compare_fusion.4, f32[4,32]{1,0:T(4,128)S(1)} %get-tuple-element.188, s32[]{:T(128)} %get-tuple-element.179), kind=kOutput, calls=%fused_computation.6.clone.1 | convolution fusion | flops 12582912 | bytes 1180164 | tf_op jit(solution)/shard_map/while/body/eval_jaxpr/cmk,c->mk/dot_general | solution.py:56
  108.4 2.2 %fusion.21 = f32[1,128,256]{2,0,1:T(1,128)S(1)} fusion(pred[32,128,256]{2,1,0:T(32,128)(4,1)S(1)} %iota_compare_fusion.4, f32[4,32]{1,0:T(4,128)S(1)} %get-tuple-element.188, s32[]{:T(128)} %get-tuple-element.179), kind=kOutput, calls=%fused_computation.6.clone.1 | convolution fusion | flops 12582912 | bytes 1180164 | tf_op jit(solution)/shard_map/while/body/eval_jaxpr/cmk,c->mk/dot_general | solution.py:56
  110.6 1.8 dynamic_update_slice.91
  115.2 57.4 %reduce-scatter.3.cloned.1.call-done = f32[16,1024]{1,0:T(8,128)} async-done(((f32[256,1024]{1,0:T(8,128)}), f32[16,1024]{1,0:T(8,128)}) %reduce-scatter.3.cloned.1.call-update) | async-done | bytes 65552 | tf_op jit(solution)/shard_map/reduce_scatter | solution.py:125
  172.6 11.7 %reduce-scatter.5.cloned.1.call-done = f32[16,512]{1,0:T(8,128)} async-done(((f32[16,1024]{1,0:T(8,128)}), f32[16,512]{1,0:T(8,128)}) %reduce-scatter.5.cloned.1.call-update) | async-done | bytes 32784 | tf_op jit(solution)/shard_map/reduce_scatter | solution.py:126
  (121 shorter events, 38.4 us)
Async XLA Ops:
  7.2 33.7 %copy-start = (f32[128,1024]{1,0:T(8,128)S(1)}, f32[128,1024]{1,0:T(8,128)}, u32[]{:S(2)}) copy-start(f32[128,1024]{1,0:T(8,128)} %param.12) | copy-start | bytes 1572868
  19.4 12.4 %all-to-all-start.1 = ((s32[2,16,4]{2,0,1:T(2,128)}), s32[2,16,4]{2,0,1:T(2,128)S(1)}, u32[]{:S(2)}, u32[]{:S(2)}) async-start(s32[2,16,4]{2,0,1:T(2,128)} %copy.43), calls=%async_computation.1 | async-start | bytes 32768 | tf_op jit(solution)/shard_map/all_to_all | solution.py:75
  26.2 5.7 %copy-start.1 = (s32[128,128]{1,0:T(8,128)S(1)}, s32[128,128]{1,0:T(8,128)}, u32[]{:S(2)}) copy-start(s32[128,128]{1,0:T(8,128)} %param.13) | copy-start | bytes 196612
  33.3 7.4 %all-to-all-start.2 = ((f32[2,16,4,128]{3,2,1,0:T(4,128)}), f32[2,16,4,128]{3,2,1,0:T(4,128)S(1)}, u32[]{:S(2)}, u32[]{:S(2)}) async-start(f32[2,16,4,128]{3,2,1,0:T(4,128)} %bitcast.13), calls=%async_computation.2 | async-start | bytes 131072 | tf_op jit(solution)/shard_map/all_to_all | solution.py:118
  40.8 8.9 %collective-permute-start = (f32[2,1,4,128]{3,2,1,0:T(4,128)S(1)}, f32[2,1,4,128]{3,2,1,0:T(4,128)S(1)}, u32[]{:S(2)}, u32[]{:S(2)}) collective-permute-start(f32[2,1,4,128]{3,2,1,0:T(4,128)S(1)} %get-tuple-element.99), channel_id=1, source_target_pairs={{0,1},{1,0},{2,3},{3,2},{4,5},{5,4},{6,7},{7,6},{8,9},{9,8},{10,11... | collective-permute-start | bytes 12296 | tf_op jit(solution)/shard_map/ppermute | solution.py:102
  42.6 26.6 %all-to-all-start.3 = ((f32[2,16,4,1024]{3,2,1,0:T(4,128)}), f32[2,16,4,1024]{3,2,1,0:T(4,128)S(1)}, u32[]{:S(2)}, u32[]{:S(2)}) async-start(f32[2,16,4,1024]{3,2,1,0:T(4,128)} %reshape.118), calls=%async_computation.3 | async-start | bytes 1048576 | tf_op jit(solution)/shard_map/all_to_all | solution.py:112
  46.1 4.0 %collective-permute-start.1 = (f32[2,1,4,128]{3,2,1,0:T(4,128)S(1)}, f32[2,1,4,128]{3,2,1,0:T(4,128)S(1)}, u32[]{:S(2)}, u32[]{:S(2)}) collective-permute-start(f32[2,1,4,128]{3,2,1,0:T(4,128)S(1)} %get-tuple-element.98), channel_id=1, source_target_pairs={{0,2},{1,3},{2,0},{3,1},{4,6},{5,7},{6,4},{7,5},{8,10},{9,11},{10,... | collective-permute-start | bytes 12296 | tf_op jit(solution)/shard_map/ppermute | solution.py:102
  46.7 5.8 %collective-permute-start.2 = (f32[2,1,4,128]{3,2,1,0:T(4,128)S(1)}, f32[2,1,4,128]{3,2,1,0:T(4,128)S(1)}, u32[]{:S(2)}, u32[]{:S(2)}) collective-permute-start(f32[2,1,4,128]{3,2,1,0:T(4,128)S(1)} %get-tuple-element.97), channel_id=1, source_target_pairs={{0,3},{1,2},{2,1},{3,0},{4,7},{5,6},{6,5},{7,4},{8,11},{9,10},{10,... | collective-permute-start | bytes 12296 | tf_op jit(solution)/shard_map/ppermute | solution.py:102
  48.0 4.9 %collective-permute-start.3 = (f32[2,1,4,128]{3,2,1,0:T(4,128)S(1)}, f32[2,1,4,128]{3,2,1,0:T(4,128)S(1)}, u32[]{:S(2)}, u32[]{:S(2)}) collective-permute-start(f32[2,1,4,128]{3,2,1,0:T(4,128)S(1)} %get-tuple-element.96), channel_id=1, source_target_pairs={{0,4},{1,5},{2,6},{3,7},{4,0},{5,1},{6,2},{7,3},{8,12},{9,13},{10,... | collective-permute-start | bytes 12296 | tf_op jit(solution)/shard_map/ppermute | solution.py:102
  48.5 6.6 %collective-permute-start.4 = (f32[2,1,4,128]{3,2,1,0:T(4,128)S(1)}, f32[2,1,4,128]{3,2,1,0:T(4,128)S(1)}, u32[]{:S(2)}, u32[]{:S(2)}) collective-permute-start(f32[2,1,4,128]{3,2,1,0:T(4,128)S(1)} %get-tuple-element.95), channel_id=1, source_target_pairs={{0,5},{1,4},{2,7},{3,6},{4,1},{5,0},{6,3},{7,2},{8,13},{9,12},{10,... | collective-permute-start | bytes 12296 | tf_op jit(solution)/shard_map/ppermute | solution.py:102
  49.7 5.8 %collective-permute-start.5 = (f32[2,1,4,128]{3,2,1,0:T(4,128)S(1)}, f32[2,1,4,128]{3,2,1,0:T(4,128)S(1)}, u32[]{:S(2)}, u32[]{:S(2)}) collective-permute-start(f32[2,1,4,128]{3,2,1,0:T(4,128)S(1)} %get-tuple-element.94), channel_id=1, source_target_pairs={{0,6},{1,7},{2,4},{3,5},{4,2},{5,3},{6,0},{7,1},{8,14},{9,15},{10,... | collective-permute-start | bytes 12296 | tf_op jit(solution)/shard_map/ppermute | solution.py:102
  50.2 8.5 %collective-permute-start.6 = (f32[2,1,4,128]{3,2,1,0:T(4,128)S(1)}, f32[2,1,4,128]{3,2,1,0:T(4,128)S(1)}, u32[]{:S(2)}, u32[]{:S(2)}) collective-permute-start(f32[2,1,4,128]{3,2,1,0:T(4,128)S(1)} %get-tuple-element.93), channel_id=1, source_target_pairs={{0,7},{1,6},{2,5},{3,4},{4,3},{5,2},{6,1},{7,0},{8,15},{9,14},{10,... | collective-permute-start | bytes 12296 | tf_op jit(solution)/shard_map/ppermute | solution.py:102
  52.4 6.8 %collective-permute-start.7 = (f32[2,1,4,128]{3,2,1,0:T(4,128)S(1)}, f32[2,1,4,128]{3,2,1,0:T(4,128)S(1)}, u32[]{:S(2)}, u32[]{:S(2)}) collective-permute-start(f32[2,1,4,128]{3,2,1,0:T(4,128)S(1)} %get-tuple-element.92), channel_id=1, source_target_pairs={{0,8},{1,9},{2,10},{3,11},{4,12},{5,13},{6,14},{7,15},{8,0},{9,1},... | collective-permute-start | bytes 12296 | tf_op jit(solution)/shard_map/ppermute | solution.py:102
  52.9 9.2 %collective-permute-start.8 = (f32[2,1,4,128]{3,2,1,0:T(4,128)S(1)}, f32[2,1,4,128]{3,2,1,0:T(4,128)S(1)}, u32[]{:S(2)}, u32[]{:S(2)}) collective-permute-start(f32[2,1,4,128]{3,2,1,0:T(4,128)S(1)} %get-tuple-element.91), channel_id=1, source_target_pairs={{0,9},{1,8},{2,11},{3,10},{4,13},{5,12},{6,15},{7,14},{8,1},{9,0},... | collective-permute-start | bytes 12296 | tf_op jit(solution)/shard_map/ppermute | solution.py:102
  55.0 7.8 %collective-permute-start.9 = (f32[2,1,4,128]{3,2,1,0:T(4,128)S(1)}, f32[2,1,4,128]{3,2,1,0:T(4,128)S(1)}, u32[]{:S(2)}, u32[]{:S(2)}) collective-permute-start(f32[2,1,4,128]{3,2,1,0:T(4,128)S(1)} %get-tuple-element.90), channel_id=1, source_target_pairs={{0,10},{1,11},{2,8},{3,9},{4,14},{5,15},{6,12},{7,13},{8,2},{9,3},... | collective-permute-start | bytes 12296 | tf_op jit(solution)/shard_map/ppermute | solution.py:102
  55.6 11.2 %collective-permute-start.10 = (f32[2,1,4,128]{3,2,1,0:T(4,128)S(1)}, f32[2,1,4,128]{3,2,1,0:T(4,128)S(1)}, u32[]{:S(2)}, u32[]{:S(2)}) collective-permute-start(f32[2,1,4,128]{3,2,1,0:T(4,128)S(1)} %get-tuple-element.89), channel_id=1, source_target_pairs={{0,11},{1,10},{2,9},{3,8},{4,15},{5,14},{6,13},{7,12},{8,3},{9,2},... | collective-permute-start | bytes 12296 | tf_op jit(solution)/shard_map/ppermute | solution.py:102
  58.7 8.0 %collective-permute-start.11 = (f32[2,1,4,128]{3,2,1,0:T(4,128)S(1)}, f32[2,1,4,128]{3,2,1,0:T(4,128)S(1)}, u32[]{:S(2)}, u32[]{:S(2)}) collective-permute-start(f32[2,1,4,128]{3,2,1,0:T(4,128)S(1)} %get-tuple-element.88), channel_id=1, source_target_pairs={{0,12},{1,13},{2,14},{3,15},{4,8},{5,9},{6,10},{7,11},{8,4},{9,5},... | collective-permute-start | bytes 12296 | tf_op jit(solution)/shard_map/ppermute | solution.py:102
  59.2 7.5 %collective-permute-start.12 = (f32[2,1,4,128]{3,2,1,0:T(4,128)S(1)}, f32[2,1,4,128]{3,2,1,0:T(4,128)S(1)}, u32[]{:S(2)}, u32[]{:S(2)}) collective-permute-start(f32[2,1,4,128]{3,2,1,0:T(4,128)S(1)} %get-tuple-element.87), channel_id=1, source_target_pairs={{0,13},{1,12},{2,15},{3,14},{4,9},{5,8},{6,11},{7,10},{8,5},{9,4},... | collective-permute-start | bytes 12296 | tf_op jit(solution)/shard_map/ppermute | solution.py:102
  62.2 6.3 %collective-permute-start.13 = (f32[2,1,4,128]{3,2,1,0:T(4,128)S(1)}, f32[2,1,4,128]{3,2,1,0:T(4,128)S(1)}, u32[]{:S(2)}, u32[]{:S(2)}) collective-permute-start(f32[2,1,4,128]{3,2,1,0:T(4,128)S(1)} %get-tuple-element.86), channel_id=1, source_target_pairs={{0,14},{1,15},{2,12},{3,13},{4,10},{5,11},{6,8},{7,9},{8,6},{9,7},... | collective-permute-start | bytes 12296 | tf_op jit(solution)/shard_map/ppermute | solution.py:102
  62.8 5.7 %collective-permute-start.14 = (f32[2,1,4,128]{3,2,1,0:T(4,128)S(1)}, f32[2,1,4,128]{3,2,1,0:T(4,128)S(1)}, u32[]{:S(2)}, u32[]{:S(2)}) collective-permute-start(f32[2,1,4,128]{3,2,1,0:T(4,128)S(1)} %get-tuple-element.85), channel_id=1, source_target_pairs={{0,15},{1,14},{2,13},{3,12},{4,11},{5,10},{6,9},{7,8},{8,7},{9,6},... | collective-permute-start | bytes 12296 | tf_op jit(solution)/shard_map/ppermute | solution.py:102
  70.1 19.9 %all-to-all-start.4 = ((f32[2,16,4,1024]{3,2,0,1:T(4,128)}), f32[2,16,4,1024]{3,2,0,1:T(4,128)S(1)}, u32[]{:S(2)}, u32[]{:S(2)}) async-start(f32[2,16,4,1024]{3,2,0,1:T(4,128)} %copy.48), calls=%async_computation.4 | async-start | bytes 1048576 | tf_op jit(solution)/shard_map/all_to_all | solution.py:111
  75.6 97.0 %reduce-scatter.3.cloned.1.call-start = ((), (), s32[]{:S(2)}) async-start(), calls=%async_computation.7 | async-start | bytes 1114112 | tf_op jit(solution)/shard_map/reduce_scatter | solution.py:125
  90.3 0.8 copy-start.2
  115.1 69.2 %reduce-scatter.5.cloned.1.call-start = ((), (), s32[]{:S(2)}) async-start(), calls=%async_computation.8 | async-start | bytes 98304 | tf_op jit(solution)/shard_map/reduce_scatter | solution.py:126
Sparse Core Ops, SparseCore 0:
  115.2 57.2 reduce-scatter.2
  175.4 8.8 reduce-scatter.4
